TPU v7x, 32 devices: a whole 2x2x4 slice. The times are simulated.
32 devices in a mesh: row: 4 (over z), col: 8 (over y, x, core).
Axes of the slice: x: 2, y: 2, z: 4, core: 2. Of those that a mesh axis runs over, the one named last changes fastest.
Arguments:
- a_matrix: float32 [16384, 16384], P('row', 'col'), may hold values from -2.25 to 2.25
- b_matrix: float32 [16384, 16384], P('row', 'col'), may hold values from -0.1 to 3.1
- x_block: float32 [16384, 64], P('row'), may hold values from -6 to 6
- r_block: float32 [16384, 64], P('row'), may hold values from -6 to 6
- p_block: float32 [16384, 64], P('row'), may hold values from -6 to 6
Outputs:
- x_next: float32 [16384, 64], P('row')
- r_next: float32 [16384, 64], P('row')
- p_next: float32 [16384, 64], P('row')
All inputs are finite; a program needn't handle non-finite values.
Results may differ from a plain program's by a relative error of at most 0.0003.
Values sent between devices are 32-bit elements; how exact they have to be, the bound alone decides.
A program may use at most 192 MiB of HBM per device.

v0:
```python
import math

import jax
import jax.numpy as jnp
from jax import lax
from jax.sharding import PartitionSpec as P

N = 16384
ITERS = 2
NS_STEPS = 8


def spread(value, axis, source):
    kept = jnp.where(lax.axis_index(axis) == source, value, 0).astype(value.dtype)
    return lax.psum(kept, axis)


def matmul(left, right):
    return jnp.dot(left, right, precision=lax.Precision.HIGHEST, preferred_element_type=jnp.float32)


def ritz_step(gram_a, gram_b, count):
    gram_a = 0.5 * (gram_a + gram_a.T)
    gram_b = 0.5 * (gram_b + gram_b.T)
    lower = jnp.linalg.cholesky(gram_b)
    half = lax.linalg.triangular_solve(lower, gram_a, left_side=True, lower=True)
    middle = lax.linalg.triangular_solve(lower, half.T, left_side=True, lower=True)
    middle = 0.5 * (middle + middle.T)
    extent = middle.shape[0]
    ident = jnp.eye(extent, dtype=middle.dtype)
    shift = jnp.trace(middle) / extent
    centred = middle - shift * ident
    sign_est = centred / jnp.sqrt(jnp.sum(centred * centred) + 1e-06)
    for turn in range(NS_STEPS):
        sign_est = 1.5 * sign_est - 0.5 * matmul(sign_est, matmul(sign_est, sign_est))
    filtered = (0.5 * (ident - sign_est))[:, :count]
    coords = lax.linalg.triangular_solve(
        lower, filtered, left_side=True, lower=True, transpose_a=True
    ) * math.sqrt(N)
    reduced = matmul(filtered.T, matmul(middle, filtered))
    return (coords, reduced)


def local(a_matrix, b_matrix, x_block, r_block, p_block):
    ratio = lax.axis_size("col") // lax.axis_size("row")
    col_index = lax.axis_index("col")
    tile_cols = a_matrix.shape[1]
    width = x_block.shape[1]
    for turn in range(ITERS):
        panel = jnp.concatenate([x_block, r_block, p_block], axis=1)
        own_part = lax.dynamic_slice_in_dim(panel, col_index % ratio * tile_cols, tile_cols, 0)
        matched = spread(own_part, "row", col_index // ratio)
        products = lax.psum(
            jnp.concatenate([matmul(a_matrix, matched), matmul(b_matrix, matched)], axis=1), "col"
        )
        grams = lax.psum(matmul(panel.T, products), "row")
        coords, reduced = ritz_step(grams[:, : 3 * width], grams[:, 3 * width :], width)
        new_resid = matmul(products[:, : 3 * width], coords) - matmul(
            matmul(products[:, 3 * width :], coords), reduced
        )
        x_block = matmul(panel, coords)
        p_block = matmul(panel[:, width:], coords[width:])
        r_block = new_resid
    return (x_block, r_block, p_block)


def solution(mesh):
    return jax.shard_map(
        local,
        mesh=mesh,
        in_specs=(P("row", "col"), P("row", "col"), P("row", None), P("row", None), P("row", None)),
        out_specs=(P("row", None), P("row", None), P("row", None)),
        check_vma=False,
    )
```

profile of v0, /device:TPU:0, one launch (start us, length us, event | category | flops | bytes accessed | tf_op | source)
XLA Modules:
  0.0 861.8 jit_solution(8819377317058890777)
XLA Ops:
  7.2 1.3 constant_dynamic-update-slice_fusion.2
  8.6 1.3 constant_dynamic-update-slice_fusion.1
  9.9 1.3 constant_dynamic-update-slice_fusion
  11.2 1.3 dynamic-slice_select_fusion.1
  12.5 71.8 %all-reduce.12.cloned.1.call-done = f32[2048,192]{0,1:T(8,128)} async-done(((f32[2048,192]{0,1:T(8,128)}), f32[2048,192]{0,1:T(8,128)}) %all-reduce.12.cloned.1.call-update) | async-done | bytes 1572880 | tf_op jit(solution)/shard_map/psum | solution.py:15
  84.3 40.1 %convolution_bitcast_fusion.2 = f32[4096,192]{0,1:T(8,128)S(1)} fusion(f32[2048,192]{0,1:T(8,128)} %all-reduce.12.cloned.1.call-done, f32[4096,2048]{1,0:T(8,128)} %param.11), kind=kOutput, calls=%fused_computation.4 | convolution fusion | flops 19327352832 | bytes 38273024 | tf_op jit(solution)/shard_map/dot_general | solution.py:19
  124.4 37.8 %convolution_bitcast_fusion.3 = f32[4096,192]{0,1:T(8,128)S(1)} fusion(f32[2048,192]{0,1:T(8,128)S(1)} %copy-done.2, f32[4096,2048]{1,0:T(8,128)} %param.10), kind=kOutput, calls=%fused_computation.5 | convolution fusion | flops 19327352832 | bytes 38273024 | tf_op jit(solution)/shard_map/dot_general | solution.py:19
  162.2 3.1 pad_maximum_fusion
  165.3 103.2 %all-reduce.14.cloned.1.call-done = f32[4096,384]{0,1:T(8,128)} async-done(((f32[4096,384]{0,1:T(8,128)}), f32[4096,384]{0,1:T(8,128)}) %all-reduce.14.cloned.1.call-update) | async-done | bytes 6291472 | tf_op jit(solution)/shard_map/psum | solution.py:53
  268.5 9.2 %fusion.104 = f32[192,384]{1,0:T(8,128)} fusion(f32[4096,192]{0,1:T(8,128)S(1)} %constant_dynamic-update-slice_fusion, f32[4096,384]{0,1:T(8,128)} %all-reduce.14.cloned.1.call-done), kind=kOutput, calls=%fused_computation.191 | convolution fusion | flops 3623878656 | bytes 9732096 | tf_op jit(solution)/shard_map/dot_general | solution.py:19
  278.0 35.9 %all-reduce.16.cloned.1.call-done = f32[192,384]{1,0:T(8,128)} async-done(((f32[192,384]{1,0:T(8,128)}), f32[192,384]{1,0:T(8,128)}) %all-reduce.16.cloned.1.call-update) | async-done | bytes 294928 | tf_op jit(solution)/shard_map/psum | solution.py:56
  313.9 1.8 slice.231
  315.7 1.7 copy.8
  317.4 1.9 fusion.42
  319.3 1.7 copy.10
  323.4 1.6 copy.11
  325.0 13.2 %cholesky.136 = f32[128,128]{1,0:T(8,128)} custom-call(f32[128,128]{1,0:T(8,128)} %copy.11), custom_call_target="Cholesky" | custom-call | tf_op jit(solution)/shard_map/jit(cholesky)/cholesky | solution.py:25
  338.1 1.5 select_reduce_fusion.3
  339.6 1.5 cholesky.165
  341.2 11.3 %custom-call.19 = f32[1,128,128]{1,2,0:T(8,128)} custom-call(f32[1,128,128]{2,1,0:T(8,128)} %get-tuple-element.81), custom_call_target="InvertDiagBlocksLowerTriangular" | custom-call | tf_op jit(solution)/shard_map/jit(cholesky)/cholesky | solution.py:25
  352.4 1.8 constant_dynamic-update-slice_fusion.6
  354.2 1.5 convolution_subtract_fusion.9
  355.7 1.5 copy.13
  357.2 6.6 cholesky.156
  369.4 21.5 %custom-call.22 = f32[2,128,128]{1,2,0:T(8,128)} custom-call(f32[2,128,128]{2,1,0:T(8,128)} %pad_maximum_fusion.5), custom_call_target="InvertDiagBlocksLowerTriangular" | custom-call | tf_op jit(solution)/shard_map/triangular_solve/custom-call.4 | solution.py:37
  390.9 1.7 copy.14
  397.3 1.2 fusion.47
  398.7 1.2 convolution_subtract_fusion.5
  402.3 1.6 select_reduce_fusion.1
  417.2 2.2 fusion.100
  419.7 1.5 fusion.8
  421.2 7.0 fusion.4
  428.2 2.2 fusion.6
  430.4 2.5 convolution_subtract_fusion.1
  433.1 1.3 dynamic-slice_select_fusion
  434.5 68.8 %all-reduce.18.cloned.1.call-done = f32[2048,192]{0,1:T(8,128)} async-done(((f32[2048,192]{0,1:T(8,128)}), f32[2048,192]{0,1:T(8,128)}) %all-reduce.18.cloned.1.call-update) | async-done | bytes 1572880 | tf_op jit(solution)/shard_map/psum | solution.py:15
  503.4 40.5 %convolution_bitcast_fusion = f32[4096,192]{0,1:T(8,128)S(1)} fusion(f32[2048,192]{0,1:T(8,128)} %all-reduce.18.cloned.1.call-done, f32[4096,2048]{1,0:T(8,128)} %param.11), kind=kOutput, calls=%fused_computation.2 | convolution fusion | flops 19327352832 | bytes 38273024 | tf_op jit(solution)/shard_map/dot_general | solution.py:19
  543.9 37.6 %convolution_bitcast_fusion.1 = f32[4096,192]{0,1:T(8,128)S(1)} fusion(f32[2048,192]{0,1:T(8,128)S(1)} %copy-done.3, f32[4096,2048]{1,0:T(8,128)} %param.10), kind=kOutput, calls=%fused_computation.3 | convolution fusion | flops 19327352832 | bytes 38273024 | tf_op jit(solution)/shard_map/dot_general | solution.py:19
  581.4 3.1 pad_maximum_fusion.1
  584.6 103.2 %all-reduce.20.cloned.1.call-done = f32[4096,384]{0,1:T(8,128)} async-done(((f32[4096,384]{0,1:T(8,128)}), f32[4096,384]{0,1:T(8,128)}) %all-reduce.20.cloned.1.call-update) | async-done | bytes 6291472 | tf_op jit(solution)/shard_map/psum | solution.py:53
  687.8 9.3 %fusion.101 = f32[192,384]{1,0:T(8,128)} fusion(f32[4096,384]{0,1:T(8,128)} %all-reduce.20.cloned.1.call-done, f32[4096,64]{0,1:T(8,128)S(1)} %fusion.8, f32[4096,64]{0,1:T(8,128)S(1)} %convolution_subtract_fusion.1, f32[4096,64]{0,1:T(8,128)S(1)} %copy-done.1), kind=kOutput, calls=%fused_computation.190 | convolution fusion | flops 3625451520 | bytes 9732096 | tf_op jit(solution)/shard_map/dot_general | solution.py:19
  697.1 36.2 %all-reduce.22.cloned.1.call-done = f32[192,384]{1,0:T(8,128)} async-done(((f32[192,384]{1,0:T(8,128)}), f32[192,384]{1,0:T(8,128)}) %all-reduce.22.cloned.1.call-update) | async-done | bytes 294928 | tf_op jit(solution)/shard_map/psum | solution.py:56
  733.3 1.8 slice.248
  735.1 1.7 copy.18
  736.8 1.9 bitcast_add_fusion.3
  738.8 1.7 copy.19
  740.5 1.6 broadcast_multiply_fusion
  742.1 1.7 copy.20
  746.2 13.2 %cholesky.174 = f32[128,128]{1,0:T(8,128)} custom-call(f32[128,128]{1,0:T(8,128)} %cholesky.211), custom_call_target="Cholesky" | custom-call | tf_op jit(solution)/shard_map/jit(cholesky)/cholesky | solution.py:25
  759.4 1.5 cholesky.203
  760.9 1.5 select_reduce_fusion.2
  762.4 11.3 %custom-call.23 = f32[1,128,128]{1,2,0:T(8,128)} custom-call(f32[1,128,128]{2,1,0:T(8,128)} %get-tuple-element.79), custom_call_target="InvertDiagBlocksLowerTriangular" | custom-call | tf_op jit(solution)/shard_map/jit(cholesky)/cholesky | solution.py:25
  773.6 1.7 constant_dynamic-update-slice_fusion.4
  775.3 1.5 convolution_subtract_fusion.7
  776.8 6.6 cholesky.194
  789.0 21.3 %custom-call.26 = f32[2,128,128]{1,2,0:T(8,128)} custom-call(f32[2,128,128]{2,1,0:T(8,128)} %pad_maximum_fusion.6), custom_call_target="InvertDiagBlocksLowerTriangular" | custom-call | tf_op jit(solution)/shard_map/triangular_solve/custom-call.4 | solution.py:37
  810.3 1.7 copy.21
  816.8 1.2 fusion.45
  821.1 1.6 select_reduce_fusion
  836.0 3.1 fusion.99
  839.2 2.7 fusion.12
  842.2 7.0 fusion
  849.1 2.2 fusion.2
  851.3 3.5 convolution_subtract_fusion
  (143 shorter events, 53.3 us)
Async XLA Ops:
  7.2 77.1 %all-reduce.12.cloned.1.call-start = ((), (), s32[]{:S(2)}) async-start(), calls=%async_computation | async-start | bytes 3145728 | tf_op jit(solution)/shard_map/psum | solution.py:15
  12.5 256.0 %all-reduce.14.cloned.1.call-start = ((), (), s32[]{:S(2)}) async-start(), calls=%async_computation.1 | async-start | bytes 12582912 | tf_op jit(solution)/shard_map/psum | solution.py:53
  84.3 40.1 %copy-start.2 = (f32[2048,192]{0,1:T(8,128)S(1)}, f32[2048,192]{0,1:T(8,128)}, u32[]{:S(2)}) copy-start(f32[2048,192]{0,1:T(8,128)} %all-reduce.12.cloned.1.call-done) | copy-start | bytes 4718596
  165.3 148.6 %all-reduce.16.cloned.1.call-start = ((), (), s32[]{:S(2)}) async-start(), calls=%async_computation.2 | async-start | bytes 589824 | tf_op jit(solution)/shard_map/psum | solution.py:56
  277.7 225.6 %all-reduce.18.cloned.1.call-start = ((), (), s32[]{:S(2)}) async-start(), calls=%async_computation.3 | async-start | bytes 3145728 | tf_op jit(solution)/shard_map/psum | solution.py:15
  313.9 78.7 %copy-start.6 = (f32[192,384]{1,0:T(8,128)S(1)}, f32[192,384]{1,0:T(8,128)}, u32[]{:S(2)}) copy-start(f32[192,384]{1,0:T(8,128)} %all-reduce.16.cloned.1.call-done) | copy-start | bytes 884740
  322.1 0.7 copy-start.14
  368.0 0.7 copy-start.9
  396.7 0.7 copy-start.10
  400.9 0.6 copy-start.15
  408.8 6.5 copy-start.13
  412.3 8.9 %slice-start = ((s8[6291456]{0:T(1024)(128)(4,1)}), s8[4194304]{0:T(1024)(128)(4,1)S(1)}, s32[]{:S(2)}) async-start(s8[6291456]{0:T(1024)(128)(4,1)} %bitcast.196), calls=%async_computation.6 | async-start | bytes 8388608
  414.1 5.6 copy-start.4
  414.1 5.6 copy-start.5
  417.2 4.0 slice-start.1
  419.4 13.5 %copy-start = (f32[4096,64]{0,1:T(8,128)}, f32[4096,64]{0,1:T(8,128)S(1)}, u32[]{:S(2)}) copy-start(f32[4096,64]{0,1:T(8,128)S(1)} %fusion.100) | copy-start | bytes 3145732
  434.5 253.3 %all-reduce.20.cloned.1.call-start = ((), (), s32[]{:S(2)}) async-start(), calls=%async_computation.4 | async-start | bytes 12582912 | tf_op jit(solution)/shard_map/psum | solution.py:53
  503.4 40.5 %copy-start.3 = (f32[2048,192]{0,1:T(8,128)S(1)}, f32[2048,192]{0,1:T(8,128)}, u32[]{:S(2)}) copy-start(f32[2048,192]{0,1:T(8,128)} %all-reduce.18.cloned.1.call-done) | copy-start | bytes 4718596
  584.5 103.3 %copy-start.1 = (f32[4096,64]{0,1:T(8,128)S(1)}, f32[4096,64]{0,1:T(8,128)}, u32[]{:S(2)}) copy-start(f32[4096,64]{0,1:T(8,128)} %copy-done) | copy-start | bytes 3145732
  584.5 148.8 %all-reduce.22.cloned.1.call-start = ((), (), s32[]{:S(2)}) async-start(), calls=%async_computation.5 | async-start | bytes 589824 | tf_op jit(solution)/shard_map/psum | solution.py:56
  733.3 78.7 %copy-start.7 = (f32[192,384]{1,0:T(8,128)S(1)}, f32[192,384]{1,0:T(8,128)}, u32[]{:S(2)}) copy-start(f32[192,384]{1,0:T(8,128)} %all-reduce.22.cloned.1.call-done) | copy-start | bytes 884740
  744.9 0.7 copy-start.16
  787.6 0.7 copy-start.8
  816.1 0.7 copy-start.11
  827.6 6.4 copy-start.12
  831.1 11.0 %slice-start.2 = ((s8[6291456]{0:T(1024)(128)(4,1)}), s8[4194304]{0:T(1024)(128)(4,1)S(1)}, s32[]{:S(2)}) async-start(s8[6291456]{0:T(1024)(128)(4,1)} %bitcast.198), calls=%async_computation.8 | async-start | bytes 8388608
  836.0 6.1 slice-start.3
Sparse Core Ops, SparseCore 0:
  12.6 71.6 all-reduce.11
  165.4 103.0 all-reduce.13
  277.8 36.0 all-reduce.15
  434.6 68.7 all-reduce.17
  584.7 103.0 all-reduce.19
  697.3 36.0 all-reduce.21
where the time goes:
time: 870 us; the launch traced here: 862 us
  waiting for transfers between devices  419 us (48%)
  matrix products  251 us (29%)
  other arithmetic  138 us (16%)
  local copies, waits for them, and re-layouts  33.3 us (4%)
  between operations  20.3 us (2%)
    dot_general x52, matrix products, matmul(): jnp.dot(left, right, precision=lax.Precision.HIGHEST, preferred_element_t...  228 us
    psum x2, waiting for transfers between devices, local(): lax.psum(jnp.concatenate([matmul(a_matrix, matched), matmul(b_matrix, mat...  206 us
    psum x2, waiting for transfers between devices, spread(): return lax.psum(kept, axis)  141 us
    psum x2, waiting for transfers between devices, local(): grams = lax.psum(matmul(panel.T, products), 'row')  72.1 us
    another operation x14, other arithmetic, ritz_step(): lower = jnp.linalg.cholesky(gram_b)  68.9 us
    another operation x10, other arithmetic, ritz_step(): lax.linalg.triangular_solve(lower, filtered, left_side=True, lower=True,...  46.2 us
  transfers between devices with their start and end apart: 6, of which 6 were waited for; matrix products, arithmetic and copies ran while one was open for 0% of the time, Pallas kernels for 0%

commit v1 on v0

v1 whole, which is shorter than its diff:
```python
import functools
import math

import jax
import jax.numpy as jnp
from jax import lax
from jax.experimental import pallas as pl
from jax.experimental.pallas import tpu as pltpu
from jax.sharding import PartitionSpec as P

NS_STEPS = 8
HIGHEST = lax.Precision.HIGHEST
HIGH = lax.Precision.HIGH


def mm(left, right, lc=1, rc=0, precision=HIGHEST):
    return lax.dot_general(
        left, right, (((lc,), (rc,)), ((), ())), precision=precision, preferred_element_type=jnp.float32
    )


def total(value):
    return lax.psum(lax.psum(value, "row"), "col")


def spread_t(value_t, tile_cols):
    ratio = lax.axis_size("col") // lax.axis_size("row")
    col_index = lax.axis_index("col")
    part = lax.dynamic_slice_in_dim(value_t, col_index % ratio * tile_cols, tile_cols, 1)
    kept = jnp.where(lax.axis_index("row") == col_index // ratio, part, 0.0)
    return lax.psum(kept, "row")


def block_inverse(block):
    size = block.shape[0]
    rows = lax.broadcasted_iota(jnp.int32, (size, size), 0)
    cols = lax.broadcasted_iota(jnp.int32, (size, size), 1)
    inverse = jnp.where(rows == cols, 1.0, 0.0)
    for j in range(size):
        pivot = 1.0 / block[j : j + 1, j : j + 1]
        factor = jnp.where(rows[:, :1] > j, block[:, j : j + 1], 0.0)
        inverse = inverse - factor * (inverse[j : j + 1] * pivot)
        block = block - factor * (block[j : j + 1] * pivot)
    diag = jnp.sum(jnp.where(rows == cols, block, 0.0), axis=1, keepdims=True)
    return inverse / jnp.sqrt(diag)


def ritz_kernel(order, ga_ref, gb_ref, w_ref, ch_ref, wa_ref, wb_ref, linv_ref, sym_ref):
    n, k = w_ref.shape[0], ch_ref.shape[1]
    gb = gb_ref[...]
    sym_ref[...] = 0.5 * (gb + gb.T)
    ga = ga_ref[...]
    ga = 0.5 * (ga + ga.T)
    nb = n // k
    cut = lambda ref, i, j: ref[i * k : (i + 1) * k, j * k : (j + 1) * k]
    linv_ref[...] = jnp.zeros((n, n), jnp.float32)
    low, inv = {}, {}
    for j in range(nb):
        for i in range(j, nb):
            rest = cut(sym_ref, i, j)
            for m in range(j):
                rest = rest - mm(low[i, m], low[j, m], 1, 1)
            if i == j:
                inv[j, j] = block_inverse(rest)
            else:
                low[i, j] = mm(rest, inv[j, j], 1, 1)
    for j in range(nb):
        for i in range(j + 1, nb):
            total = mm(low[i, j], inv[j, j])
            for m in range(j + 1, i):
                total = total + mm(low[i, m], inv[m, j])
            inv[i, j] = -mm(inv[i, i], total)
    for (i, j), value in inv.items():
        linv_ref[i * k : (i + 1) * k, j * k : (j + 1) * k] = value
    linv = linv_ref[...]
    linv_t = linv.T
    middle = mm(mm(linv, ga), linv_t)
    middle = 0.5 * (middle + middle.T)
    rows = lax.broadcasted_iota(jnp.int32, (n, n), 0)
    cols = lax.broadcasted_iota(jnp.int32, (n, n), 1)
    ident = jnp.where(rows == cols, 1.0, 0.0)
    shift = jnp.sum(middle * ident) / n
    centred = middle - shift * ident
    sign_est = centred / jnp.sqrt(jnp.full((1, 1), jnp.sum(centred * centred) + 1e-06))
    for turn in range(NS_STEPS):
        sign_est = 1.5 * sign_est - 0.5 * mm(sign_est, mm(sign_est, sign_est))
    filtered = (0.5 * (ident - sign_est))[:, :k]
    coords = mm(linv_t, filtered) * math.sqrt(order)
    reduced = mm(filtered.T, mm(middle, filtered))
    ch_ref[...] = mm(coords, reduced)
    w_ref[:, :k] = coords
    w_ref[:, k:] = jnp.where(lax.broadcasted_iota(jnp.int32, (n, k), 0) >= k, coords, 0.0)
    w = w_ref[...]
    w_t = w.T
    wa_ref[...] = mm(w_t, mm(ga, w))
    wb_ref[...] = mm(w_t, mm(sym_ref[...], w))


def ritz(order, width, gram_a, gram_b):
    n, k = gram_a.shape[0], width
    shape = lambda *dims: jax.ShapeDtypeStruct(dims, jnp.float32)
    return pl.pallas_call(
        functools.partial(ritz_kernel, order),
        out_shape=(shape(n, 2 * k), shape(n, k), shape(2 * k, 2 * k), shape(2 * k, 2 * k)),
        in_specs=[pl.BlockSpec(memory_space=pltpu.VMEM)] * 2,
        out_specs=[pl.BlockSpec(memory_space=pltpu.VMEM)] * 4,
        scratch_shapes=[pltpu.VMEM((n, n), jnp.float32)] * 2,
        name="ritz",
    )(gram_a, gram_b)


def extend(kept, fresh):
    k = fresh.shape[1]
    x, r, p = fresh[:k], fresh[k : 2 * k], fresh[2 * k :]
    return jnp.concatenate(
        [
            jnp.concatenate([kept[:k, :k], x, kept[:k, k:]], axis=1),
            jnp.concatenate([x.T, r, p.T], axis=1),
            jnp.concatenate([kept[k:, :k], p, kept[k:, k:]], axis=1),
        ],
        axis=0,
    )


def local(order, a_matrix, b_matrix, x_block, r_block, p_block):
    tile_cols = a_matrix.shape[1]
    k = x_block.shape[1]
    panel = jnp.concatenate([x_block, r_block, p_block], axis=1)
    matched_t = spread_t(panel.T, tile_cols)
    prod_a = mm(a_matrix, matched_t, 1, 1, HIGH)
    prod_b = mm(b_matrix, matched_t, 1, 1, HIGH)
    grams = total(jnp.concatenate([mm(panel, prod_a, 0, 0), mm(panel, prod_b, 0, 0)], axis=1))
    w, ch, kept_a, kept_b = ritz(order, k, grams[:, : 3 * k], grams[:, 3 * k :])
    coords = w[:, :k]
    resid_t = lax.psum(mm(coords, prod_a, 0, 1) - mm(ch, prod_b, 0, 1), "col")
    matched_t = spread_t(resid_t, tile_cols)
    both = mm(panel, w)
    panel = jnp.concatenate([both[:, :k], resid_t.T, both[:, k:]], axis=1)
    fresh_a = mm(a_matrix, matched_t, 1, 1, HIGH)
    fresh_b = mm(b_matrix, matched_t, 1, 1, HIGH)
    grams = total(jnp.concatenate([mm(panel, fresh_a, 0, 0), mm(panel, fresh_b, 0, 0)], axis=1))
    w2, ch2, _, _ = ritz(order, k, extend(kept_a, grams[:, :k]), extend(kept_b, grams[:, k:]))
    c2 = w2[:, :k]
    outer = lambda c: jnp.concatenate([c[:k], c[2 * k :]], axis=0)
    on_a, on_b = mm(w, outer(c2)), mm(w, outer(ch2))
    resid_t = lax.psum(
        (mm(on_a, prod_a, 0, 1) + mm(c2[k : 2 * k], fresh_a, 0, 1))
        - (mm(on_b, prod_b, 0, 1) + mm(ch2[k : 2 * k], fresh_b, 0, 1)),
        "col",
    )
    both = mm(panel, w2)
    return (both[:, :k], resid_t.T, both[:, k:])


def solution(mesh):
    def whole(a_matrix, b_matrix, x_block, r_block, p_block):
        return jax.shard_map(
            functools.partial(local, a_matrix.shape[0]),
            mesh=mesh,
            in_specs=(P("row", "col"), P("row", "col"), P("row", None), P("row", None), P("row", None)),
            out_specs=(P("row", None), P("row", None), P("row", None)),
            check_vma=False,
        )(a_matrix, b_matrix, x_block, r_block, p_block)

    return whole
```

time: 870 us -> 641 us (0.74)
  other arithmetic: 138 us -> 9.16 us
  matrix products: 251 us -> 134 us
  Pallas kernels: 0 us -> 59 us
  waiting for transfers between devices: 419 us -> 393 us
  local copies, waits for them, and re-layouts: 33.3 us -> 22.6 us
    another operation x26 -> x0, other arithmetic: 115 us -> none  [the longest x14 68.9 us: ritz_step(): lower = jnp.linalg.cholesky(gram_b)]
    dot_general x52 -> x18, matrix products: 228 us -> 134 us  [mm(): lax.dot_general(left, right, (((lc,), (rc,)), ((), ())), precision=precis...]
    pallas_call x0 -> x2, Pallas kernels: none -> 59 us  [ritz(): pl.pallas_call(functools.partial(ritz_kernel, order), out_shape=(shape(n,...]
    psum x6 -> x8, waiting for transfers between devices: 419 us -> 393 us  [the longest x4 180 us: total(): return lax.psum(lax.psum(value, 'row'), 'col')]
    another operation x22 -> x0, matrix products: 22.1 us -> none  [the longest x6 6.81 us: ritz_step(): lax.linalg.triangular_solve(lower, half.T, left_side=True, lower=True)]
    another operation x13 -> x0, local copies, waits for them, and re-layouts: 9.13 us -> none  [the longest x6 7.34 us: ritz_step(): lower = jnp.linalg.cholesky(gram_b)]
  transfers between devices with their start and end apart: 6 -> 8, of which waited for: 6 -> 8; matrix products, arithmetic and copies ran while one was open for 0% -> 2% of each run, Pallas kernels for 0% -> 0%
where the time goes in v1:
time: 641 us; the launch traced here: 633 us
  waiting for transfers between devices  393 us (61%)
  matrix products  134 us (21%)
  Pallas kernels  59 us (9%)
  local copies, waits for them, and re-layouts  22.6 us (4%)
  between operations  14.6 us (2%)
  other arithmetic  9.16 us (1%)
    psum x4, waiting for transfers between devices, total(): return lax.psum(lax.psum(value, 'row'), 'col')  180 us
    dot_general x18, matrix products, mm(): lax.dot_general(left, right, (((lc,), (rc,)), ((), ())), precision=precis...  134 us
    psum x2, waiting for transfers between devices, spread_t(): return lax.psum(kept, 'row')  106 us
    pallas_call x2, Pallas kernels, ritz(): pl.pallas_call(functools.partial(ritz_kernel, order), out_shape=(shape(n,...  59 us
    psum x1, waiting for transfers between devices, local(): lax.psum(mm(on_a, prod_a, 0, 1) + mm(c2[k:2 * k], fresh_a, 0, 1) - (mm(on...  54.7 us
    psum x1, waiting for transfers between devices, local(): resid_t = lax.psum(mm(coords, prod_a, 0, 1) - mm(ch, prod_b, 0, 1), 'col')  51.4 us
  transfers between devices with their start and end apart: 8, of which 8 were waited for; matrix products, arithmetic and copies ran while one was open for 2% of the time, Pallas kernels for 0%

profile of v1, /device:TPU:0, one launch (start us, length us, event | category | flops | bytes accessed | tf_op | source)
XLA Modules:
  0.0 632.8 jit_solution(8663134355446850811)
XLA Ops:
  7.2 1.3 constant_dynamic-update-slice_fusion.2
  8.6 1.3 constant_dynamic-update-slice_fusion.1
  9.9 1.3 constant_dynamic-update-slice_fusion
  11.2 1.5 select_bitcast_fusion
  12.7 0.0 all-reduce.11.cloned.1.call-start
  12.7 0.6 copy-done.2
  13.3 71.2 %all-reduce.9.cloned.1.call-done = f32[192,2048]{1,0:T(8,128)} async-done(((f32[192,2048]{1,0:T(8,128)}), f32[192,2048]{1,0:T(8,128)}) %all-reduce.9.cloned.1.call-update) | async-done | bytes 1572880 | tf_op jit(solution)/shard_map/psum | solution.py:31
  84.5 20.8 %fusion.32 = f32[192,4096]{1,0:T(8,128)S(1)} fusion(f32[192,2048]{1,0:T(8,128)} %all-reduce.9.cloned.1.call-done, f32[4096,2048]{1,0:T(8,128)} %param.5), kind=kOutput, calls=%fused_computation.49 | convolution fusion | flops 9663676416 | bytes 38273024 | tf_op jit(solution)/shard_map/dot_general | solution.py:17
  105.3 4.6 fusion.33
  109.9 22.2 %fusion.34 = f32[192,4096]{1,0:T(8,128)} fusion(f32[192,2048]{1,0:T(8,128)} %all-reduce.9.cloned.1.call-done, f32[4096,2048]{1,0:T(8,128)} %param.6), kind=kOutput, calls=%fused_computation.51 | convolution fusion | flops 9663676416 | bytes 38273024 | tf_op jit(solution)/shard_map/dot_general | solution.py:17
  132.1 5.5 fusion.35
  137.6 0.8 pad_maximum_fusion.4
  138.5 35.2 %all-reduce.11.cloned.1.call-done = f32[192,384]{1,0:T(8,128)} async-done(((f32[192,384]{1,0:T(8,128)}), f32[192,384]{1,0:T(8,128)}) %all-reduce.11.cloned.1.call-update) | async-done | bytes 294928 | tf_op jit(solution)/shard_map/psum | solution.py:23
  173.8 56.2 %all-reduce.13.cloned.1.call-done = f32[192,384]{1,0:T(8,128)} async-done(((f32[192,384]{1,0:T(8,128)}), f32[192,384]{1,0:T(8,128)}) %all-reduce.13.cloned.1.call-update) | async-done | bytes 294928 | tf_op jit(solution)/shard_map/psum | solution.py:23
  230.0 1.8 fusion.24
  231.8 29.4 %ritz.2 = (f32[192,128]{1,0:T(8,128)}, f32[192,64]{1,0:T(8,128)}, f32[128,128]{1,0:T(8,128)}, f32[128,128]{1,0:T(8,128)}) custom-call(f32[192,192]{1,0:T(8,128)} %get-tuple-element.20.ga_ref, f32[192,192]{1,0:T(8,128)} %get-tuple-element.19.gb_ref), custom_call_target="tpu_custom_call" | custom-call | tf_op jit(solution)/shard_map/ritz/pallas_call | solution.py:102
  261.2 3.3 fusion.5
  264.6 3.1 convolution_subtract_fusion
  267.7 0.0 all-reduce.17.cloned.1.call-start
  267.7 5.5 fusion.36
  273.2 51.4 %all-reduce.15.cloned.1.call-done = f32[64,4096]{1,0:T(8,128)} async-done(((f32[64,4096]{1,0:T(8,128)}), f32[64,4096]{1,0:T(8,128)}) %all-reduce.15.cloned.1.call-update) | async-done | bytes 1048592 | tf_op jit(solution)/shard_map/psum | solution.py:135
  324.7 1.9 dynamic-slice_select_fusion
  326.6 0.0 all-reduce.19.cloned.1.call-start
  326.6 3.1 fusion.23
  329.7 0.1 copy.13
  329.8 0.7 fusion.29
  330.5 34.9 %all-reduce.17.cloned.1.call-done = f32[64,2048]{1,0:T(8,128)} async-done(((f32[64,2048]{1,0:T(8,128)}), f32[64,2048]{1,0:T(8,128)}) %all-reduce.17.cloned.1.call-update) | async-done | bytes 524304 | tf_op jit(solution)/shard_map/psum | solution.py:31
  365.4 22.1 %fusion.37 = f32[64,4096]{1,0:T(8,128)} fusion(f32[64,2048]{1,0:T(8,128)} %all-reduce.17.cloned.1.call-done, f32[4096,2048]{1,0:T(8,128)} %param.5), kind=kOutput, calls=%fused_computation.54 | convolution fusion | flops 3221225472 | bytes 35127296 | tf_op jit(solution)/shard_map/dot_general | solution.py:17
  387.5 5.3 fusion.4
  392.7 22.3 %fusion.38 = f32[64,4096]{1,0:T(8,128)} fusion(f32[64,2048]{1,0:T(8,128)} %all-reduce.17.cloned.1.call-done, f32[4096,2048]{1,0:T(8,128)} %param.6), kind=kOutput, calls=%fused_computation.55 | convolution fusion | flops 3221225472 | bytes 35127296 | tf_op jit(solution)/shard_map/dot_general | solution.py:17
  415.0 5.3 fusion.3
  420.3 0.7 pad_maximum_fusion.5
  421.0 0.0 all-reduce.21.cloned.1.call-start
  421.0 0.6 fusion.28
  421.7 0.1 copy.10
  421.7 33.8 %all-reduce.19.cloned.1.call-done = f32[192,128]{0,1:T(8,128)} async-done(((f32[192,128]{0,1:T(8,128)}), f32[192,128]{0,1:T(8,128)}) %all-reduce.19.cloned.1.call-update) | async-done | bytes 98320 | tf_op jit(solution)/shard_map/psum | solution.py:23
  455.6 0.4 all-reduce.23.cloned.1.call-start
  456.1 0.7 fusion.31
  456.8 55.0 %all-reduce.21.cloned.1.call-done = f32[192,128]{0,1:T(8,128)} async-done(((f32[192,128]{0,1:T(8,128)}), f32[192,128]{0,1:T(8,128)}) %all-reduce.21.cloned.1.call-update) | async-done | bytes 98320 | tf_op jit(solution)/shard_map/psum | solution.py:23
  511.8 1.5 fusion.25
  513.3 0.1 copy.21
  513.4 0.1 copy.16
  513.5 0.8 pad_maximum_fusion.6
  514.3 0.7 copy.17
  515.0 0.7 copy.18
  515.7 0.8 copy.20
  516.6 0.9 pad_maximum_fusion.8
  517.4 0.1 copy.12
  517.5 1.4 copy.9
  519.0 1.0 maximum_maximum_fusion
  520.0 0.8 copy.19.ga_ref
  520.7 1.7 maximum_maximum_fusion.1.gb_ref
  522.4 29.6 %ritz.3 = (f32[192,128]{1,0:T(8,128)}, f32[192,64]{1,0:T(8,128)}, f32[128,128]{1,0:T(8,128)}, f32[128,128]{1,0:T(8,128)}) custom-call(f32[192,192]{1,0:T(8,128)} %copy.19.ga_ref, f32[192,192]{1,0:T(8,128)} %maximum_maximum_fusion.1.gb_ref), custom_call_target="tpu_custom_call" | custom-call | tf_op jit(solution)/shard_map/ritz/pallas_call | solution.py:102
  552.0 0.9 fusion.27
  553.0 5.6 fusion.2
  558.5 0.2 fusion.11
  558.8 2.1 fusion.40
  560.9 0.2 fusion.7
  561.2 2.1 fusion.39
  563.3 1.8 convolution_add_fusion.1
  565.2 2.1 fusion.1
  567.3 1.5 fusion.22
  568.8 54.7 %all-reduce.23.cloned.1.call-done = f32[4096,64]{0,1:T(8,128)} async-done(((f32[4096,64]{0,1:T(8,128)}), f32[4096,64]{0,1:T(8,128)}) %all-reduce.23.cloned.1.call-update) | async-done | bytes 1048592 | tf_op jit(solution)/shard_map/psum | solution.py:146
  623.5 2.3 copy.32
  (37 shorter events, 0.3 us)
Async XLA Ops:
  7.2 77.3 %all-reduce.9.cloned.1.call-start = ((), (), s32[]{:S(2)}) async-start(), calls=%async_computation | async-start | bytes 3145728 | tf_op jit(solution)/shard_map/psum | solution.py:31
  11.2 2.1 copy-start.2
  12.7 161.1 %all-reduce.11.cloned.1.call-start = ((), (), s32[]{:S(2)}) async-start(), calls=%async_computation.1 | async-start | bytes 589824 | tf_op jit(solution)/shard_map/psum | solution.py:23
  138.5 91.5 %all-reduce.13.cloned.1.call-start = ((), (), s32[]{:S(2)}) async-start(), calls=%async_computation.2 | async-start | bytes 589824 | tf_op jit(solution)/shard_map/psum | solution.py:23
  173.7 150.9 %all-reduce.15.cloned.1.call-start = ((), (), s32[]{:S(2)}) async-start(), calls=%async_computation.3 | async-start | bytes 2097152 | tf_op jit(solution)/shard_map/psum | solution.py:135
  261.2 3.3 copy-start
  261.2 3.3 copy-start.12
  264.6 3.2 copy-start.6
  267.7 97.7 %all-reduce.17.cloned.1.call-start = ((), (), s32[]{:S(2)}) async-start(), calls=%async_computation.4 | async-start | bytes 1048576 | tf_op jit(solution)/shard_map/psum | solution.py:31
  273.2 56.5 %copy-start.10 = (f32[128,128]{1,0:T(8,128)S(1)}, f32[128,128]{1,0:T(8,128)}, u32[]{:S(2)}) copy-start(f32[128,128]{1,0:T(8,128)} %get-tuple-element.12) | copy-start | bytes 196612
  273.2 56.6 %copy-start.9 = (f32[128,128]{1,0:T(8,128)S(1)}, f32[128,128]{1,0:T(8,128)}, u32[]{:S(2)}) copy-start(f32[128,128]{1,0:T(8,128)} %get-tuple-element.11) | copy-start | bytes 196612
  326.6 129.0 %all-reduce.19.cloned.1.call-start = ((), (), s32[]{:S(2)}) async-start(), calls=%async_computation.5 | async-start | bytes 262144 | tf_op jit(solution)/shard_map/psum | solution.py:23
  421.0 90.8 %all-reduce.21.cloned.1.call-start = ((), (), s32[]{:S(2)}) async-start(), calls=%async_computation.6 | async-start | bytes 262144 | tf_op jit(solution)/shard_map/psum | solution.py:23
  455.6 167.9 %all-reduce.23.cloned.1.call-start = ((), (), s32[]{:S(2)}) async-start(), calls=%async_computation.7 | async-start | bytes 2097152 | tf_op jit(solution)/shard_map/psum | solution.py:146
  513.4 3.2 copy-start.7
  516.6 2.4 copy-start.8
  552.0 6.5 %copy-start.11 = (f32[192,64]{1,0:T(8,128)S(1)}, f32[192,64]{1,0:T(8,128)}, u32[]{:S(2)}) copy-start(f32[192,64]{1,0:T(8,128)} %get-tuple-element.14) | copy-start | bytes 147460
  552.0 6.8 %copy-start.1 = (f32[192,4096]{1,0:T(8,128)S(1)}, f32[192,4096]{1,0:T(8,128)}, u32[]{:S(2)}) copy-start(f32[192,4096]{1,0:T(8,128)} %fusion.34) | copy-start | bytes 9437188
  560.9 2.4 copy-start.3
  561.2 4.0 copy-start.4
  565.2 2.1 copy-start.5
Sparse Core Ops, SparseCore 0:
  12.8 71.6 all-reduce.8
  138.6 35.0 all-reduce.10
  176.8 53.0 all-reduce.12
  267.8 56.8 all-reduce.14
  327.5 37.8 all-reduce.16
  421.1 34.4 all-reduce.18
  458.6 53.1 all-reduce.20
  567.4 56.0 all-reduce.22
